TPU v7x, 256 devices: a whole 4x4x8 slice. The times are simulated.
256 devices in a mesh: region: 16 (over z_lo, x, core), member: 16 (over y, z_hi).
Axes of the slice: x: 4, y: 4, z: 8 (z_hi: 4, z_lo: 2; z = z_hi * 2 + z_lo), core: 2. Of those that a mesh axis runs over, the one named last changes fastest.
Arguments:
- predicted_states: float32 [32, 100, 512, 128], P('member', None, 'region'), may hold values from -20 to 20, as said below
- observed_analysis: float32 [100, 512, 128], P(None, 'region'), may hold values from -20 to 20
- tile_location_sequence: int32 [16, 4096], P('region'), may hold values from 0 to 4095, each once within a row
Outputs:
- gradient: float32 [32, 100, 512, 128], P('member', None, 'region')
Inputs may be any that keep to these rules, and one draw needn't show every extreme that they name: Each row of tile_location_sequence is a permutation of the cells of one region. `predicted_states`: members share a common field per variable and cell, with variable and cell scales.
All inputs are finite; a program needn't handle non-finite values.
Results may differ from a plain program's by a relative error of at most 0.0003.
Values sent between devices are 32-bit elements; how exact they have to be, the bound alone decides.
A program may use at most 128 MiB of HBM per device.

v0:
```python
import jax
import jax.numpy as jnp
from jax import lax
from jax.sharding import PartitionSpec as P

LON = 128
HALF = 32
PATCH = 128


def extended(block, sides, width):
    for axis, dim in sides:
        count = lax.axis_size(axis)
        forward = [(i, i + 1) for i in range(count - 1)]
        backward = [(target, source) for source, target in forward]
        low = lax.ppermute(
            lax.slice_in_dim(block, block.shape[dim] - width, None, axis=dim), axis, forward
        )
        high = lax.ppermute(lax.slice_in_dim(block, 0, width, axis=dim), axis, backward)
        block = jnp.concatenate([low, block, high], axis=dim)
    return block


def kernel_value(offset, half):
    sigma = half / 2.0
    steps = jnp.arange(-half, half + 1).astype(jnp.float32)
    norm_sum = jnp.sum(jnp.exp(-(steps * steps) / (2.0 * sigma * sigma)))
    bell = jnp.exp(-(offset * offset) / (2.0 * sigma * sigma)) / norm_sum
    value = 0.5 * (offset == 0.0).astype(jnp.float32) + 0.5 * bell
    return jnp.where(jnp.abs(offset) <= half, value, jnp.zeros_like(value))


def lon_matrix():
    first = jnp.arange(LON)[:, None]
    second = jnp.arange(LON)[None, :]
    offset = second - first
    return kernel_value(offset.astype(jnp.float32), HALF)


def band_rows(along_lon):
    padded = extended(along_lon, (("region", 2),), HALF)
    local_rows = along_lon.shape[2]
    out_rows = jnp.arange(local_rows)[:, None]
    in_rows = jnp.arange(local_rows + 2 * HALF)[None, :]
    lat_band = kernel_value((in_rows - HALF - out_rows).astype(jnp.float32), HALF)
    return jnp.einsum("rp,mvpk->mvrk", lat_band, padded, precision=lax.Precision.HIGHEST)


def smooth_surface(values):
    along_lon = jnp.einsum("mvrl,lk->mvrk", values, lon_matrix(), precision=lax.Precision.HIGHEST)
    return band_rows(along_lon)


def pair_terms(gathered):
    members = gathered.shape[0]
    inner_products = jnp.einsum(
        "mvkp,nvkp->vkmn", gathered, gathered, precision=lax.Precision.HIGHEST
    )
    squares = jnp.einsum("mvkp,mvkp->vkm", gathered, gathered, precision=lax.Precision.HIGHEST)
    dist_sq = jnp.maximum(
        squares[:, :, :, None] + squares[:, :, None, :] - 2.0 * inner_products, 0.0
    )
    self_pair = jnp.arange(members)[:, None] == jnp.arange(members)[None, :]
    pair_weights = jnp.where(
        self_pair[None, None], jnp.zeros_like(dist_sq), 1.0 / jnp.sqrt(dist_sq + 1e-06)
    )
    pulled = jnp.transpose(jnp.sum(pair_weights, axis=-1), (2, 0, 1))
    apart = pulled[..., None] * gathered - jnp.einsum(
        "vkmn,nvkp->mvkp", pair_weights, gathered, precision=lax.Precision.HIGHEST
    )
    apart = apart / members
    return lax.all_to_all(apart, "member", split_axis=0, concat_axis=2, tiled=True)


def reorder_cells(values, positions):
    cell_count = values.shape[-1]
    flattened = values.reshape(-1, cell_count).T
    reordered = jnp.take(flattened, positions, axis=0)
    return reordered.T.reshape(values.shape)


def on_device(predicted_states, observed_analysis, tile_location_sequence):
    local_ensemble_copies = predicted_states.shape[0]
    quantity_names = predicted_states.shape[1]
    mesh_locations = predicted_states.shape[2] * predicted_states.shape[3]
    blocks = mesh_locations // PATCH
    order = tile_location_sequence[0]
    inverse_order = (
        jnp.zeros((mesh_locations,), jnp.int32).at[order].set(jnp.arange(mesh_locations))
    )
    softened_surface = smooth_surface(predicted_states)
    picked = reorder_cells(
        softened_surface.reshape(local_ensemble_copies, quantity_names, mesh_locations), order
    )
    picked = picked.reshape(local_ensemble_copies, quantity_names, blocks, PATCH)
    truth = reorder_cells(observed_analysis.reshape(quantity_names, mesh_locations), order).reshape(
        quantity_names, blocks, PATCH
    )
    diff = picked - truth[None]
    toward = diff / jnp.sqrt(jnp.sum(diff * diff, axis=-1, keepdims=True) + 1e-06)
    apart = pair_terms(lax.all_to_all(picked, "member", split_axis=2, concat_axis=0, tiled=True))
    patch_grad = jnp.sqrt(jnp.float32(PATCH)) * (toward - apart)
    located_points = reorder_cells(
        patch_grad.reshape(local_ensemble_copies, quantity_names, mesh_locations), inverse_order
    )
    return smooth_surface(located_points.reshape(predicted_states.shape))


def solution(mesh):
    in_specs = (P("member", None, "region", None), P(None, "region", None), P("region", None))
    out_specs = P("member", None, "region", None)
    return jax.shard_map(
        on_device, mesh=mesh, in_specs=in_specs, out_specs=out_specs, check_vma=False
    )
```

profile of v0, /device:TPU:1, one launch (start us, length us, event | category | flops | bytes accessed | tf_op | source)
XLA Modules:
  0.0 415.7 jit_solution(14891175216338866984)
XLA Ops:
  1.9 5.8 %fusion.14 = f32[2,100,32,128]{3,1,2,0:T(8,128)S(1)} fusion(f32[2,100,32,128]{3,2,1,0:T(8,128)S(1)} %copy-done, f32[]{:T(128)} %exponential_reduce_fusion), kind=kOutput, calls=%fused_computation.29 | convolution fusion | flops 1258504192 | bytes 6553604 | tf_op jit(solution)/shard_map/mvrl,lk->mvrk/dot_general | solution.py:50
  9.4 4.5 %collective-permute-start = (f32[2,100,32,128]{3,2,1,0:T(8,128)S(1)}, f32[2,100,32,128]{3,2,1,0:T(8,128)S(1)}, u32[]{:S(2)}, u32[]{:S(2)}) collective-permute-start(f32[2,100,32,128]{3,2,1,0:T(8,128)S(1)} %copy.65), channel_id=1, source_target_pairs={{0,16},{16,32},{32,48},{48,64},{64,80},{80,96},{96,112},{112,128},... | collective-permute-start | bytes 9830408 | tf_op jit(solution)/shard_map/ppermute | solution.py:16
  16.3 33.2 %collective-permute-done = f32[2,100,32,128]{3,2,1,0:T(8,128)S(1)} collective-permute-done((f32[2,100,32,128]{3,2,1,0:T(8,128)S(1)}, f32[2,100,32,128]{3,2,1,0:T(8,128)S(1)}, u32[]{:S(2)}, u32[]{:S(2)}) %collective-permute-start) | collective-permute-done | bytes 3276832 | tf_op jit(solution)/shard_map/ppermute | solution.py:16
  49.5 3.6 copy.67
  53.9 3.7 copy.68
  57.7 8.5 %pad_maximum_fusion = f32[2,100,96,128]{3,1,2,0:T(8,128)} fusion(f32[2,100,32,128]{3,1,2,0:T(8,128)} %copy.68, f32[2,100,32,128]{3,1,2,0:T(8,128)} %copy-done.2, f32[2,100,32,128]{3,1,2,0:T(8,128)} %copy.67), kind=kLoop, calls=%fused_computation.4 | loop fusion | flops 4915200 | bytes 19660800 | tf_op jit(solution)/shard_map/concatenate | solution.py:20
  66.2 10.9 %fusion.6 = f32[2,100,128,32]{2,3,1,0:T(8,128)S(1)} fusion(f32[2,100,96,128]{3,1,2,0:T(8,128)} %pad_maximum_fusion, f32[]{:T(128)} %exponential_reduce_fusion, s32[96]{0:T(128)S(1)} %iota_add_fusion), kind=kOutput, calls=%fused_computation.11 | convolution fusion | flops 943758336 | bytes 13107588 | tf_op jit(solution)/shard_map/rp,mvpk->mvrk/dot_general | solution.py:46
  80.0 3.3 copy.70
  83.3 18.3 %gather_fusion.1 = f32[4096,200]{1,0:T(8,128)} fusion(f32[4096,200]{1,0:T(8,128)} %bitcast.86, s32[4096]{0:T(1024)S(1)} %fusion.25), kind=kCustom, calls=%fused_computation.clone | custom fusion | bytes 6569984 | tf_op jit(solution)/shard_map/jit(_take)/gather | solution.py:78
  101.6 3.7 copy.71
  107.9 4.2 %copy.74 = f32[2,100,32,128]{3,0,1,2:T(2,128)} copy(f32[2,100,32,128]{3,2,1,0:T(8,128)S(1)} %bitcast.91) | data formatting | bytes 6553600 | tf_op jit(solution)/shard_map/reshape;reshape | solution.py:95
  112.1 11.4 %all-to-all-start = ((f32[2,100,32,128]{3,0,1,2:T(2,128)}), f32[2,100,32,128]{3,0,1,2:T(2,128)S(1)}, u32[]{:S(2)}, u32[]{:S(2)}) async-start(f32[2,100,32,128]{3,0,1,2:T(2,128)} %copy.74), calls=%async_computation | async-start | bytes 6553600 | tf_op jit(solution)/shard_map/all_to_all | solution.py:101
  123.5 54.1 %all-to-all-done = f32[2,100,32,128]{3,0,1,2:T(2,128)S(1)} async-done(((f32[2,100,32,128]{3,0,1,2:T(2,128)}), f32[2,100,32,128]{3,0,1,2:T(2,128)S(1)}, u32[]{:S(2)}, u32[]{:S(2)}) %all-to-all-start) | async-done | bytes 3276832 | tf_op jit(solution)/shard_map/all_to_all | solution.py:101
  182.5 6.2 %fusion.46 = (f32[100,2,32]{2,1,0:T(2,128)S(1)}, f32[100,2,32,32]{2,3,1,0:T(8,128)S(1)}) fusion(f32[32,100,2,128]{3,0,2,1:T(8,128)S(1)} %bitcast.89, f32[100,2,32]{2,1,0:T(2,128)S(1)} %multiply_reduce_fusion, pred[32,32]{0,1:T(8,128)(4,1)S(1)} %iota_compare_fusion), kind=kOutput, calls=%fused_computation.74 | convolution fusion | flops 316000000 | bytes 4148224 | tf_op jit(solution)/shard_map/mvkp,nvkp->vkmn/dot_general | solution.py:56
  188.7 6.6 %fusion.13 = f32[32,100,2,128]{3,0,2,1:T(8,128)S(1)} fusion(f32[32,100,2,128]{3,0,2,1:T(8,128)S(1)} %bitcast.90, f32[100,2,32,32]{2,3,1,0:T(8,128)S(1)} %get-tuple-element.7, f32[32,100,2]{0,2,1:T(2,128)S(1)} %bitcast.102), kind=kOutput, calls=%fused_computation.23 | convolution fusion | flops 317030400 | bytes 7398400 | tf_op jit(solution)/shard_map/vkmn,nvkp->mvkp/dot_general | solution.py:68
  195.3 4.2 %copy.78 = f32[32,100,2,128]{3,2,1,0:T(2,128)} copy(f32[32,100,2,128]{3,0,2,1:T(8,128)S(1)} %fusion.13) | data formatting | bytes 6553600 | tf_op jit(solution)/shard_map/div | solution.py:71
  199.6 4.5 %all-to-all-start.1 = ((f32[32,100,2,128]{3,2,1,0:T(2,128)}), f32[32,100,2,128]{3,2,1,0:T(2,128)}, u32[]{:S(2)}, u32[]{:S(2)}) async-start(f32[32,100,2,128]{3,2,1,0:T(2,128)} %copy.78), calls=%async_computation.1 | async-start | bytes 6553600 | tf_op jit(solution)/shard_map/all_to_all | solution.py:72
  206.0 14.1 %gather_fusion = f32[4096,100]{1,0:T(8,128)} fusion(f32[4096,100]{1,0:T(8,128)S(1)} %bitcast.87, s32[4096]{0:T(1024)S(1)} %broadcast_clamp_fusion), kind=kCustom, calls=%fused_computation.2 | custom fusion | bytes 3293184 | tf_op jit(solution)/shard_map/jit(_take)/gather | solution.py:78
  220.1 4.8 %broadcast_select_fusion = f32[4096,100]{1,0:T(8,128)} fusion(f32[4096,100]{1,0:T(8,128)} %gather_fusion, pred[4096]{0:T(1024)(128)(4,1)S(1)} %compare_and_fusion.1), kind=kLoop, calls=%fused_computation.31 | loop fusion | flops 409600 | bytes 3280896 | tf_op jit(solution)/shard_map/jit(_take)/select_n | solution.py:78
  228.0 15.7 %scatter_custom_fusion = s32[4096]{0:T(1024)S(1)} fusion(s32[4096]{0:T(1024)S(1)} %bitcast.106, s32[4096]{0:T(1024)S(1)} %iota.49, s32[]{:T(128)} %constant.26.clone.1), kind=kCustom, calls=%fused_computation.53 | custom fusion | bytes 16388 | tf_op jit(solution)/shard_map/scatter | solution.py:89
  246.2 3.8 copy.106
  250.0 4.3 %all_to_all.33 = f32[200,4096]{1,0:T(8,128)} reshape(f32[2,100,16,2,128]{4,3,2,1,0:T(2,128)S(1)} %bitcast.97) | data formatting | bytes 6553600 | tf_op jit(solution)/shard_map/all_to_all | solution.py:72
  258.0 8.6 %fusion.12 = f32[4096,200]{0,1:T(8,128)} fusion(f32[200,4096]{1,0:T(8,128)S(1)} %copy-done.8, f32[25,8,32,128]{3,2,1,0:T(8,128)S(1)} %bitcast.98, f32[25,8,32,128]{3,2,1,0:T(8,128)S(1)} %bitcast.99, f32[4096,200]{0,1:T(8,128)S(1)} %copy-done.6, pred[4096]{0:T(1024)(128)(4,1)S(1)} %compare_and_fusion.1), kind=kLoop, calls=%fused_computation.19 | loop fusion | flops 4096000 | bytes 16388096 | tf_op jit(solution)/shard_map/transpose | solution.py:77
  266.6 5.2 %copy.80 = f32[4096,200]{1,0:T(8,128)} copy(f32[4096,200]{0,1:T(8,128)} %fusion.12) | data formatting | bytes 6553600 | tf_op jit(solution)/shard_map/transpose | solution.py:77
  271.8 18.3 %gather_fusion.2 = f32[4096,200]{1,0:T(8,128)} fusion(f32[4096,200]{1,0:T(8,128)} %copy.80, s32[4096]{0:T(1024)S(1)} %fusion.26), kind=kCustom, calls=%fused_computation.1.clone | custom fusion | bytes 6569984 | tf_op jit(solution)/shard_map/jit(_take)/gather | solution.py:78
  290.1 3.9 select_bitcast_fusion
  294.0 5.3 %copy.81 = f32[200,4096]{1,0:T(8,128)} copy(f32[200,4096]{0,1:T(8,128)} %select_bitcast_fusion) | data formatting | bytes 6553600 | tf_op jit(solution)/shard_map/transpose | solution.py:79
  301.8 3.4 fusion.20
  305.2 61.9 %collective-permute-start.2 = (f32[2,100,32,128]{3,2,1,0:T(8,128)S(1)}, f32[2,100,32,128]{3,2,1,0:T(8,128)S(1)}, u32[]{:S(2)}, u32[]{:S(2)}) collective-permute-start(f32[2,100,32,128]{3,2,1,0:T(8,128)S(1)} %fusion.20), channel_id=1, source_target_pairs={{0,16},{16,32},{32,48},{48,64},{64,80},{80,96},{96,112},{112,128},... | collective-permute-start | bytes 9830408 | tf_op jit(solution)/shard_map/ppermute | solution.py:16
  369.1 33.7 %collective-permute-done.2 = f32[2,100,32,128]{3,2,1,0:T(8,128)S(1)} collective-permute-done((f32[2,100,32,128]{3,2,1,0:T(8,128)S(1)}, f32[2,100,32,128]{3,2,1,0:T(8,128)S(1)}, u32[]{:S(2)}, u32[]{:S(2)}) %collective-permute-start.2) | collective-permute-done | bytes 3276832 | tf_op jit(solution)/shard_map/ppermute | solution.py:16
  402.8 4.4 %collective-permute-done.3 = f32[2,100,32,128]{3,2,1,0:T(8,128)S(1)} collective-permute-done((f32[2,100,32,128]{3,2,1,0:T(8,128)S(1)}, f32[2,100,32,128]{3,2,1,0:T(8,128)S(1)}, u32[]{:S(2)}, u32[]{:S(2)}) %collective-permute-start.3) | collective-permute-done | bytes 3276832 | tf_op jit(solution)/shard_map/ppermute | solution.py:19
  407.2 8.0 %fusion.17 = f32[2,100,32,128]{3,2,1,0:T(8,128)} fusion(f32[2,100,32,128]{3,2,1,0:T(8,128)S(1)} %collective-permute-done.3, f32[2,100,32,128]{3,2,1,0:T(8,128)S(1)} %fusion.20, f32[2,100,32,128]{3,2,1,0:T(8,128)S(1)} %collective-permute-done.2, f32[]{:T(128)} %exponential_reduce_fusion, s32[96]{0:T(128)S(1)} %iota_add_fusion), kind=kOutput, calls=%fused_computation.30 | convolution fusion | flops 948673536 | bytes 13107588 | tf_op jit(solution)/shard_map/rp,mvpk->mvrk/dot_general | solution.py:46
  (48 shorter events, 32.3 us)
Async XLA Ops:
  0.0 1.9 copy-start
  7.7 1.7 copy-start.2
  7.7 8.5 %copy-start.9 = (s32[1,4096]{1,0:T(1,128)S(1)}, s32[1,4096]{1,0:T(1,128)}, u32[]{:S(2)}) copy-start(s32[1,4096]{1,0:T(1,128)} %param.7) | copy-start | bytes 49156
  9.4 40.1 %collective-permute-start = (f32[2,100,32,128]{3,2,1,0:T(8,128)S(1)}, f32[2,100,32,128]{3,2,1,0:T(8,128)S(1)}, u32[]{:S(2)}, u32[]{:S(2)}) collective-permute-start(f32[2,100,32,128]{3,2,1,0:T(8,128)S(1)} %copy.65), channel_id=1, source_target_pairs={{0,16},{16,32},{32,48},{48,64},{64,80},{80,96},{96,112},{112,128},... | collective-permute-start | bytes 9830408 | tf_op jit(solution)/shard_map/ppermute | solution.py:16
  13.9 40.0 %collective-permute-start.1 = (f32[2,100,32,128]{3,2,1,0:T(8,128)S(1)}, f32[2,100,32,128]{3,2,1,0:T(8,128)S(1)}, u32[]{:S(2)}, u32[]{:S(2)}) collective-permute-start(f32[2,100,32,128]{3,2,1,0:T(8,128)S(1)} %copy.65), channel_id=1, source_target_pairs={{16,0},{32,16},{48,32},{64,48},{80,64},{96,80},{112,96},{128,112},... | collective-permute-start | bytes 9830408 | tf_op jit(solution)/shard_map/ppermute | solution.py:19
  105.3 1.7 copy-start.5
  107.9 4.2 %copy-start.3 = (f32[25,8,32,128]{3,2,1,0:T(8,128)}, f32[25,8,32,128]{3,2,1,0:T(8,128)S(1)}, u32[]{:S(2)}) copy-start(f32[25,8,32,128]{3,2,1,0:T(8,128)S(1)} %copy.92) | copy-start | bytes 9830404
  112.1 65.5 %all-to-all-start = ((f32[2,100,32,128]{3,0,1,2:T(2,128)}), f32[2,100,32,128]{3,0,1,2:T(2,128)S(1)}, u32[]{:S(2)}, u32[]{:S(2)}) async-start(f32[2,100,32,128]{3,0,1,2:T(2,128)} %copy.74), calls=%async_computation | async-start | bytes 6553600 | tf_op jit(solution)/shard_map/all_to_all | solution.py:101
  199.6 46.6 %all-to-all-start.1 = ((f32[32,100,2,128]{3,2,1,0:T(2,128)}), f32[32,100,2,128]{3,2,1,0:T(2,128)}, u32[]{:S(2)}, u32[]{:S(2)}) async-start(f32[32,100,2,128]{3,2,1,0:T(2,128)} %copy.78), calls=%async_computation.1 | async-start | bytes 6553600 | tf_op jit(solution)/shard_map/all_to_all | solution.py:72
  220.1 23.6 %copy-start.4 = (f32[25,8,32,128]{3,2,1,0:T(8,128)S(1)}, f32[25,8,32,128]{3,2,1,0:T(8,128)}, u32[]{:S(2)}) copy-start(f32[25,8,32,128]{3,2,1,0:T(8,128)} %copy-done.3) | copy-start | bytes 9830404
  254.3 1.4 copy-start.7
  254.3 2.4 copy-start.8
  255.2 2.7 copy-start.6
  305.2 97.5 %collective-permute-start.2 = (f32[2,100,32,128]{3,2,1,0:T(8,128)S(1)}, f32[2,100,32,128]{3,2,1,0:T(8,128)S(1)}, u32[]{:S(2)}, u32[]{:S(2)}) collective-permute-start(f32[2,100,32,128]{3,2,1,0:T(8,128)S(1)} %fusion.20), channel_id=1, source_target_pairs={{0,16},{16,32},{32,48},{48,64},{64,80},{80,96},{96,112},{112,128},... | collective-permute-start | bytes 9830408 | tf_op jit(solution)/shard_map/ppermute | solution.py:16
  367.2 40.0 %collective-permute-start.3 = (f32[2,100,32,128]{3,2,1,0:T(8,128)S(1)}, f32[2,100,32,128]{3,2,1,0:T(8,128)S(1)}, u32[]{:S(2)}, u32[]{:S(2)}) collective-permute-start(f32[2,100,32,128]{3,2,1,0:T(8,128)S(1)} %fusion.20), channel_id=1, source_target_pairs={{16,0},{32,16},{48,32},{64,48},{80,64},{96,80},{112,96},{128,112},... | collective-permute-start | bytes 9830408 | tf_op jit(solution)/shard_map/ppermute | solution.py:19
  407.2 8.0 %copy-start.1 = (f32[2,100,32,128]{3,2,1,0:T(8,128)S(1)}, f32[2,100,32,128]{3,2,1,0:T(8,128)}, u32[]{:S(2)}) copy-start(f32[2,100,32,128]{3,2,1,0:T(8,128)} %param.5) | copy-start | bytes 9830404
where the time goes:
time: 422 us; the launch traced here: 416 us
  local copies, waits for them, and re-layouts  131 us (31%)
  waiting for transfers between devices  126 us (30%)
  starting transfers between devices  86.6 us (21%)
  matrix products  41.1 us (10%)
  other arithmetic  30.3 us (7%)
    ppermute x2, waiting for transfers between devices, extended(): lax.ppermute(lax.slice_in_dim(block, block.shape[dim] - width, None, axis...  66.9 us
    ppermute x2, starting transfers between devices, extended(): lax.ppermute(lax.slice_in_dim(block, block.shape[dim] - width, None, axis...  66.4 us
    gather x4, local copies, waits for them, and re-layouts, reorder_cells(): reordered = jnp.take(flattened, positions, axis=0)  54.4 us
    all_to_all x1, waiting for transfers between devices, on_device(): lax.all_to_all(picked, 'member', split_axis=2, concat_axis=0, tiled=True)  54.1 us
    dot_general x2, matrix products, band_rows(): jnp.einsum('rp,mvpk->mvrk', lat_band, padded, precision=lax.Precision.HIG...  19 us
    scatter x1, local copies, waits for them, and re-layouts, on_device(): jnp.zeros((mesh_locations,), jnp.int32).at[order]  15.7 us
    unnamed x24, local copies, waits for them, and re-layouts  14.1 us
    all_to_all x1, starting transfers between devices, on_device(): lax.all_to_all(picked, 'member', split_axis=2, concat_axis=0, tiled=True)  11.4 us
  transfers between devices with their start and end apart: 6, of which 5 were waited for; matrix products, arithmetic and copies ran while one was open for 11% of the time, Pallas kernels for 0%

commit v1 on v0

v1 whole, which is shorter than its diff:
```python
import math

import jax
import jax.numpy as jnp
import numpy as np
from jax import lax
from jax.experimental import pallas as pl
from jax.experimental.pallas import tpu as pltpu
from jax.sharding import PartitionSpec as P

V = 100
ROWS = 32
LON = 128
HALF = 32
PATCH = 128
MEMBERS = 32
OWNERS = 16
REGIONS = 16
SLOTS = 7
SPAN = ROWS + 2 * HALF
CELLS = ROWS * LON
MESH = pl.DeviceIdType.MESH
F32 = jnp.float32
BF16 = jnp.bfloat16


def kernel_values(offset):
    sigma = HALF / 2.0
    steps = np.arange(-HALF, HALF + 1).astype(np.float64)
    norm = np.sum(np.exp(-(steps * steps) / (2.0 * sigma * sigma)))
    bell = np.exp(-(offset * offset) / (2.0 * sigma * sigma)) / norm
    value = 0.5 * (offset == 0.0) + 0.5 * bell
    return np.where(np.abs(offset) <= HALF, value, 0.0).astype(np.float32)


def halves(values):
    high = values.astype(BF16)
    low = (values - high.astype(np.float32)).astype(BF16)
    return high, low


def lat_weights():
    rows = np.arange(ROWS)[:, None]
    span = np.arange(SPAN)[None, :]
    high, low = halves(kernel_values((span - HALF - rows).astype(np.float64)))
    return np.concatenate(
        [np.concatenate([high, high], 1), np.concatenate([low, np.zeros_like(low)], 1)], 0
    )


def lon_weights():
    first = np.arange(LON)[:, None]
    second = np.arange(LON)[None, :]
    high, low = halves(kernel_values((second - first).astype(np.float64)))
    return np.concatenate(
        [np.concatenate([high, low], 1), np.concatenate([high, np.zeros_like(low)], 1)], 0
    )


def split(values):
    high = values.astype(BF16)
    low = (values - high.astype(F32)).astype(BF16)
    return high, low


def dot(a, b):
    return lax.dot_general(a, b, (((1,), (0,)), ((), ())), preferred_element_type=F32)


def dot_nt(a, b):
    return lax.dot_general(a, b, (((1,), (1,)), ((), ())), preferred_element_type=F32)


LANES = lax.GatherDimensionNumbers(
    offset_dims=(),
    collapsed_slice_dims=(1,),
    start_index_map=(1,),
    operand_batching_dims=(0,),
    start_indices_batching_dims=(0,),
)


def take_lanes(values, lanes):
    return lax.gather(
        values,
        lanes[..., None],
        LANES,
        slice_sizes=(1, 1),
        mode=lax.GatherScatterMode.PROMISE_IN_BOUNDS,
    )


def pick(src, group, row_of, lane_of, index):
    lanes = jnp.broadcast_to(lane_of[pl.ds(index, 1), :], (group, LON))
    rows = jnp.broadcast_to(row_of[pl.ds(index, 1), :], (group, LON))
    total = jnp.zeros((group, LON), F32)
    for row in range(ROWS):
        found = take_lanes(src[pl.ds(row * group, group), :], lanes)
        total = jnp.where(rows == row, found, total)
    return total


def smooth_lat(field, lat, mid):
    def pair(index, carry):
        both = jnp.concatenate([field[2 * index], field[2 * index + 1]], axis=1)
        high, low = split(both)
        parts = dot(lat[...], jnp.concatenate([high, low], axis=0))
        rows = parts[:ROWS] + parts[ROWS:]
        mid[pl.ds(pl.multiple_of(2 * index * ROWS, 64), ROWS), :] = rows[:, :LON]
        mid[pl.ds(pl.multiple_of(2 * index * ROWS + ROWS, 32), ROWS), :] = rows[:, LON:]
        return carry

    lax.fori_loop(0, MEMBERS // 2, pair, 0, unroll=2)


def smooth_lon(block, lon):
    high, low = split(block)
    parts = dot(jnp.concatenate([high, low], axis=1), lon[...])
    return parts[:, :LON] + parts[:, LON:]


def pair_block(a, truths):
    count = 4
    cube = a.reshape(count, MEMBERS, PATCH)
    mean = jnp.sum(cube, axis=1, keepdims=True) * (1.0 / MEMBERS)
    e = (cube - mean).reshape(count * MEMBERS, PATCH)
    d = (cube - truths).reshape(count * MEMBERS, PATCH)
    toward = d * lax.rsqrt(jnp.sum(d * d, axis=1, keepdims=True) + 1e-06)
    size = count * MEMBERS
    left = lax.broadcasted_iota(jnp.int32, (size, size), 0)
    right = lax.broadcasted_iota(jnp.int32, (size, size), 1)
    same = left == right
    other = jnp.logical_and(lax.div(left, MEMBERS) == lax.div(right, MEMBERS), left != right)
    high, low = split(e)
    gram = dot_nt(jnp.concatenate([high, low], axis=1), jnp.concatenate([high, high], axis=1))
    gram = gram + dot_nt(high, low)
    diagonal = jnp.where(same, gram, 0.0)
    dist = jnp.sum(diagonal, axis=1, keepdims=True) + jnp.sum(diagonal, axis=0, keepdims=True)
    dist = jnp.maximum(dist - 2.0 * gram, 0.0)
    weights = jnp.where(other, lax.rsqrt(dist + 1e-06), 0.0)
    pulled = jnp.sum(weights, axis=1, keepdims=True)
    mixing = jnp.where(same, pulled, -weights)
    mix_high, mix_low = split(mixing)
    apart = dot(jnp.concatenate([mix_high, mix_low], axis=1), jnp.concatenate([high, high], axis=0))
    apart = apart + dot(mix_high, low)
    return math.sqrt(PATCH) * (toward - apart * (1.0 / MEMBERS))


def kernel(
    x, truth, order, lat, lon, out,
    raw, grad, done, mid, cells, picked, facts, fact_rows, rows_fwd, lanes_fwd, rows_inv, lanes_inv,
    fwd_send, fwd_recv, up_send, up_recv, down_send, down_recv,
    up2_send, up2_recv, down2_send, down2_recv, ret_send, ret_recv, fact_sem,
):
    r = lax.axis_index("region")
    m = lax.axis_index("member")
    slots = jnp.where(lax.rem(m, 5) == 0, SLOTS, SLOTS - 1)
    has_low = r > 0
    has_high = r < REGIONS - 1

    def variable(slot, owner):
        return jnp.where(slot == SLOTS - 1, 96 + lax.div(owner, 5), slot * OWNERS + owner)

    barrier = pltpu.get_barrier_semaphore()
    for step in range(1, OWNERS):
        peer = (r, lax.rem(m + step, OWNERS))
        pl.semaphore_signal(barrier, inc=1, device_id=peer, device_id_type=MESH)

    @pl.when(has_low)
    def _():
        pl.semaphore_signal(barrier, inc=1, device_id=(r - 1, m), device_id_type=MESH)

    @pl.when(has_high)
    def _():
        pl.semaphore_signal(barrier, inc=1, device_id=(r + 1, m), device_id_type=MESH)

    pl.semaphore_wait(barrier, OWNERS - 1 + has_low.astype(jnp.int32) + has_high.astype(jnp.int32))

    def own_rows(slot):
        return raw.at[slot, pl.ds(2 * m, 2), pl.ds(HALF, ROWS), :]

    def send_block(slot, peer):
        pltpu.make_async_remote_copy(
            src_ref=x.at[:, variable(slot, peer)],
            dst_ref=own_rows(slot),
            send_sem=fwd_send,
            recv_sem=fwd_recv.at[slot],
            device_id=(r, peer),
            device_id_type=MESH,
        ).start()

    def send_slot(slot, carry):
        def to_peer(step, inner):
            send_block(slot, lax.rem(m + step, OWNERS))
            return inner

        return lax.fori_loop(1, OWNERS, to_peer, carry)

    lax.fori_loop(0, SLOTS - 1, send_slot, 0)
    for index in range(4):

        @pl.when(m != 5 * index)
        def _(index=index):
            send_block(SLOTS - 1, 5 * index)

    def keep_slot(slot, carry):
        pltpu.make_async_copy(x.at[:, variable(slot, m)], own_rows(slot), fwd_recv.at[slot]).start()
        pltpu.make_async_copy(truth.at[variable(slot, m)], facts.at[slot], fact_sem).start()
        return carry

    lax.fori_loop(0, slots, keep_slot, 0)

    def invert(k, carry):
        cell = order[pl.ds(k, 1), :]
        row = lax.shift_right_logical(cell, 7)
        lane = jnp.bitwise_and(cell, LON - 1)
        rows_fwd[pl.ds(k, 1), :] = row
        lanes_fwd[pl.ds(k, 1), :] = lane
        at_row = lax.broadcasted_iota(jnp.int32, (ROWS, PATCH), 0) == row
        position = lax.broadcasted_iota(jnp.int32, (ROWS, PATCH), 1).astype(F32)
        patch = jnp.where(at_row, k.astype(F32), 0.0)
        place = jnp.where(at_row, position, 0.0)
        at_lane = lax.broadcasted_iota(jnp.int32, (LON, PATCH), 0) == lane
        chosen = jnp.where(at_lane, 1.0, 0.0).astype(BF16)
        return carry + dot_nt(jnp.concatenate([patch, place], axis=0).astype(BF16), chosen)

    inverse = lax.fori_loop(0, ROWS, invert, jnp.zeros((2 * ROWS, LON), F32))
    inverse = inverse.astype(jnp.int32)
    rows_inv[...] = inverse[:ROWS]
    lanes_inv[...] = inverse[ROWS:]

    @pl.when(slots == SLOTS)
    def _():
        pltpu.make_async_copy(facts.at[pl.ds(0, 7)], facts.at[pl.ds(0, 7)], fact_sem).wait()

    @pl.when(slots != SLOTS)
    def _():
        pltpu.make_async_copy(facts.at[pl.ds(0, 6)], facts.at[pl.ds(0, 6)], fact_sem).wait()

    for row in range(ROWS):
        fact_rows[pl.ds(row * 8, 8), :] = facts[:, row, :]

    def pick_fact(k, carry):
        picked[pl.ds(pl.multiple_of(k * 8, 8), 8), :] = pick(fact_rows, 8, rows_fwd, lanes_fwd, k)
        return carry

    lax.fori_loop(0, ROWS, pick_fact, 0)
    fact_rows[...] = picked[pl.ds(0, 8 * ROWS), :]

    @pl.when(jnp.logical_not(has_low))
    def _():
        def clear(slot, carry):
            raw[slot, :, pl.ds(0, HALF), :] = jnp.zeros((MEMBERS, HALF, LON), F32)
            grad[slot, :, pl.ds(0, HALF), :] = jnp.zeros((MEMBERS, HALF, LON), F32)
            return carry

        lax.fori_loop(0, slots, clear, 0)

    @pl.when(jnp.logical_not(has_high))
    def _():
        def clear(slot, carry):
            raw[slot, :, pl.ds(HALF + ROWS, HALF), :] = jnp.zeros((MEMBERS, HALF, LON), F32)
            grad[slot, :, pl.ds(HALF + ROWS, HALF), :] = jnp.zeros((MEMBERS, HALF, LON), F32)
            return carry

        lax.fori_loop(0, slots, clear, 0)

    def send_halos(field, slot, low_send, low_recv, high_send, high_recv):
        middle = field.at[slot, :, pl.ds(HALF, ROWS), :]

        @pl.when(has_high)
        def _():
            pltpu.make_async_remote_copy(
                src_ref=middle,
                dst_ref=field.at[slot, :, pl.ds(0, HALF), :],
                send_sem=high_send,
                recv_sem=high_recv.at[slot],
                device_id=(r + 1, m),
                device_id_type=MESH,
            ).start()

        @pl.when(has_low)
        def _():
            pltpu.make_async_remote_copy(
                src_ref=middle,
                dst_ref=field.at[slot, :, pl.ds(HALF + ROWS, HALF), :],
                send_sem=low_send,
                recv_sem=low_recv.at[slot],
                device_id=(r - 1, m),
                device_id_type=MESH,
            ).start()

    def wait_halos(field, slot, low_recv, high_recv):
        @pl.when(has_low)
        def _():
            part = field.at[slot, :, pl.ds(0, HALF), :]
            pltpu.make_async_copy(part, part, high_recv.at[slot]).wait()

        @pl.when(has_high)
        def _():
            part = field.at[slot, :, pl.ds(HALF + ROWS, HALF), :]
            pltpu.make_async_copy(part, part, low_recv.at[slot]).wait()

    def arrive(slot):
        part = raw.at[slot, :, pl.ds(HALF, ROWS), :]
        pltpu.make_async_copy(part, part, fwd_recv.at[slot]).wait()
        send_halos(raw, slot, down_send, down_recv, up_send, up_recv)

    def middle(slot):
        wait_halos(raw, slot, down_recv, up_recv)
        smooth_lat(raw.at[slot], lat, mid)
        for block in range(4):
            rows = [mid[pl.ds(block * 8 + row, MEMBERS, stride=ROWS), :] for row in range(8)]
            cells[pl.ds(block * 256, 256), :] = smooth_lon(jnp.concatenate(rows, axis=0), lon)

        def pick_patch(k, carry):
            at = pl.multiple_of(k * MEMBERS, MEMBERS)
            picked[pl.ds(at, MEMBERS), :] = pick(cells, MEMBERS, rows_fwd, lanes_fwd, k)
            return carry

        lax.fori_loop(0, ROWS, pick_patch, 0)

        def quad(q, carry):
            at = pl.multiple_of(q * 4 * MEMBERS, 4 * MEMBERS)
            truths = jnp.stack(
                [fact_rows[pl.ds((4 * q + i) * 8 + slot, 1), :] for i in range(4)], axis=0
            )
            cells[pl.ds(at, 4 * MEMBERS), :] = pair_block(picked[pl.ds(at, 4 * MEMBERS), :], truths)
            return carry

        lax.fori_loop(0, ROWS // 4, quad, 0)

        def put_row(row, carry):
            grad[slot, :, HALF + row, :] = pick(cells, MEMBERS, rows_inv, lanes_inv, row)
            return carry

        lax.fori_loop(0, ROWS, put_row, 0)

    def finish(slot):
        wait_halos(grad, slot, down2_recv, up2_recv)
        smooth_lat(grad.at[slot], lat, mid)
        for block in range(4):
            part = smooth_lon(mid[pl.ds(block * 256, 256), :], lon)
            done[slot, pl.ds(block * 8, 8)] = part.reshape(8, ROWS, LON)

    def give_back(slot):
        def to_peer(step, carry):
            peer = lax.rem(m + step, OWNERS)
            pltpu.make_async_remote_copy(
                src_ref=done.at[slot, pl.ds(2 * peer, 2)],
                dst_ref=out.at[:, variable(slot, m)],
                send_sem=ret_send,
                recv_sem=ret_recv,
                device_id=(r, peer),
                device_id_type=MESH,
            ).start()
            return carry

        lax.fori_loop(1, OWNERS, to_peer, 0)
        pltpu.make_async_copy(
            done.at[slot, pl.ds(2 * m, 2)], out.at[:, variable(slot, m)], ret_recv
        ).start()

    def step(i, carry):
        @pl.when(jnp.logical_and(i >= 3, i < slots + 3))
        def _():
            give_back(i - 3)

        @pl.when(i < slots)
        def _():
            arrive(i)

        @pl.when(jnp.logical_and(i >= 1, i < slots + 1))
        def _():
            middle(i - 1)

        @pl.when(jnp.logical_and(i >= 2, i < slots + 2))
        def _():
            finish(i - 2)

        @pl.when(jnp.logical_and(i >= 1, i < slots + 1))
        def _():
            send_halos(grad, i - 1, down2_send, down2_recv, up2_send, up2_recv)

        return carry

    lax.fori_loop(0, SLOTS + 3, step, 0)

    def drain(count):
        pltpu.make_async_copy(
            x.at[:, pl.ds(0, V - count)], x.at[:, pl.ds(0, V - count)], fwd_send
        ).wait()
        sent = done.at[pl.ds(0, count), pl.ds(0, 2 * OWNERS - 2)]
        pltpu.make_async_copy(sent, sent, ret_send).wait()

        @pl.when(has_high)
        def _():
            for field, sem in ((raw, up_send), (grad, up2_send)):
                part = field.at[pl.ds(0, count), :, pl.ds(HALF, ROWS), :]
                pltpu.make_async_copy(part, part, sem).wait()

        @pl.when(has_low)
        def _():
            for field, sem in ((raw, down_send), (grad, down2_send)):
                part = field.at[pl.ds(0, count), :, pl.ds(HALF, ROWS), :]
                pltpu.make_async_copy(part, part, sem).wait()

    @pl.when(slots == SLOTS)
    def _():
        drain(SLOTS)

    @pl.when(slots != SLOTS)
    def _():
        drain(SLOTS - 1)

    pltpu.make_async_copy(out, out, ret_recv).wait()


def on_device(predicted_states, observed_analysis, tile_location_sequence):
    order = tile_location_sequence.reshape(ROWS, PATCH)
    dma = pltpu.SemaphoreType.DMA
    vmem = pl.BlockSpec(memory_space=pltpu.VMEM)
    hbm = pl.BlockSpec(memory_space=pl.ANY)
    return pl.pallas_call(
        kernel,
        out_shape=jax.ShapeDtypeStruct((2, V, ROWS, LON), F32),
        in_specs=[hbm, hbm, vmem, vmem, vmem],
        out_specs=hbm,
        scratch_shapes=[
            pltpu.VMEM((SLOTS, MEMBERS, SPAN, LON), F32),
            pltpu.VMEM((SLOTS, MEMBERS, SPAN, LON), F32),
            pltpu.VMEM((SLOTS, MEMBERS, ROWS, LON), F32),
            pltpu.VMEM((MEMBERS * ROWS, LON), F32),
            pltpu.VMEM((MEMBERS * ROWS, LON), F32),
            pltpu.VMEM((MEMBERS * ROWS, LON), F32),
            pltpu.VMEM((8, ROWS, LON), F32),
            pltpu.VMEM((8 * ROWS, LON), F32),
            pltpu.VMEM((ROWS, LON), jnp.int32),
            pltpu.VMEM((ROWS, LON), jnp.int32),
            pltpu.VMEM((ROWS, LON), jnp.int32),
            pltpu.VMEM((ROWS, LON), jnp.int32),
            dma(()), dma((SLOTS,)), dma(()), dma((SLOTS,)), dma(()), dma((SLOTS,)),
            dma(()), dma((SLOTS,)), dma(()), dma((SLOTS,)), dma(()), dma(()), dma(()),
        ],
        compiler_params=pltpu.CompilerParams(
            collective_id=0, has_side_effects=True, vmem_limit_bytes=56 * 1024 * 1024
        ),
    )(
        predicted_states,
        observed_analysis,
        order,
        jnp.asarray(lat_weights()),
        jnp.asarray(lon_weights()),
    )


def solution(mesh):
    in_specs = (P("member", None, "region", None), P(None, "region", None), P("region", None))
    out_specs = P("member", None, "region", None)
    return jax.shard_map(
        on_device, mesh=mesh, in_specs=in_specs, out_specs=out_specs, check_vma=False
    )
```

time: 422 us -> 271 us (0.64)
  the two profiles are of different devices: /device:TPU:1 before, /device:TPU:32 now
where the time goes in v1:
time: 271 us; the launch traced here: 270 us
  Pallas kernels  266 us (98%)
  local copies, waits for them, and re-layouts  3.96 us (1%)
    pallas_call x1, Pallas kernels, on_device(): pl.pallas_call(kernel, out_shape=jax.ShapeDtypeStruct((2, V, ROWS, LON),...  266 us

profile of v1, /device:TPU:32, one launch (start us, length us, event | category | flops | bytes accessed | tf_op | source)
XLA Modules:
  0.0 270.3 jit_solution(1155812558176304740)
XLA Ops:
  0.0 266.3 %shard_map.55 = f32[2,100,32,128]{3,2,1,0:T(8,128)} custom-call(f32[2,100,32,128]{3,2,1,0:T(8,128)} %x.1, f32[100,32,128]{2,1,0:T(8,128)} %truth.1, s32[32,128]{1,0:T(8,128)} %bitcast.1, bf16[64,192]{1,0:T(8,128)(2,1)} %constant.4.clone.lat, bf16[256,256]{1,0:T(8,128)(2,1)} %constant.5.clone.lon), custom_call_target="tpu_custom_call" | custom-call | tf_op jit(solution)/shard_map/pallas_call | solution.py:424
  266.3 4.0 %copy.7 = f32[2,100,32,128]{3,2,1,0:T(8,128)} copy(f32[2,100,32,128]{3,2,1,0:T(8,128)} %shard_map.55) | data formatting | bytes 6553600

commit v2 on v1

--- a/solution.py
+++ b/solution.py
@@ -158,8 +158,21 @@
     has_low = r > 0
     has_high = r < REGIONS - 1
 
+    def turned(owner, by):
+        return lax.div(owner, 4) * 4 + lax.rem(owner + 4 + by, 4)
+
     def variable(slot, owner):
-        return jnp.where(slot == SLOTS - 1, 96 + lax.div(owner, 5), slot * OWNERS + owner)
+        back = jnp.logical_and(lax.rem(slot, 2) == 1, r >= REGIONS // 2)
+        place = jnp.where(back, turned(owner, 1), owner)
+        return jnp.where(slot == SLOTS - 1, 96 + lax.div(owner, 5), slot * OWNERS + place)
+
+    def above(slot):
+        cross = jnp.logical_and(lax.rem(slot, 2) == 1, r == REGIONS // 2 - 1)
+        return (r + 1, jnp.where(cross, turned(m, -1), m))
+
+    def below(slot):
+        cross = jnp.logical_and(lax.rem(slot, 2) == 1, r == REGIONS // 2)
+        return (r - 1, jnp.where(cross, turned(m, 1), m))
 
     barrier = pltpu.get_barrier_semaphore()
     for step in range(1, OWNERS):
@@ -174,7 +187,17 @@
     def _():
         pl.semaphore_signal(barrier, inc=1, device_id=(r + 1, m), device_id_type=MESH)
 
-    pl.semaphore_wait(barrier, OWNERS - 1 + has_low.astype(jnp.int32) + has_high.astype(jnp.int32))
+    @pl.when(r == REGIONS // 2 - 1)
+    def _():
+        pl.semaphore_signal(barrier, inc=1, device_id=above(1), device_id_type=MESH)
+
+    @pl.when(r == REGIONS // 2)
+    def _():
+        pl.semaphore_signal(barrier, inc=1, device_id=below(1), device_id_type=MESH)
+
+    crossing = jnp.logical_or(r == REGIONS // 2 - 1, r == REGIONS // 2)
+    neighbours = has_low.astype(jnp.int32) + has_high.astype(jnp.int32) + crossing.astype(jnp.int32)
+    pl.semaphore_wait(barrier, OWNERS - 1 + neighbours)
 
     def own_rows(slot):
         return raw.at[slot, pl.ds(2 * m, 2), pl.ds(HALF, ROWS), :]
@@ -194,7 +217,7 @@
             send_block(slot, lax.rem(m + step, OWNERS))
             return inner
 
-        return lax.fori_loop(1, OWNERS, to_peer, carry)
+        return lax.fori_loop(1, OWNERS, to_peer, carry, unroll=5)
 
     lax.fori_loop(0, SLOTS - 1, send_slot, 0)
     for index in range(4):
@@ -224,7 +247,7 @@
         chosen = jnp.where(at_lane, 1.0, 0.0).astype(BF16)
         return carry + dot_nt(jnp.concatenate([patch, place], axis=0).astype(BF16), chosen)
 
-    inverse = lax.fori_loop(0, ROWS, invert, jnp.zeros((2 * ROWS, LON), F32))
+    inverse = lax.fori_loop(0, ROWS, invert, jnp.zeros((2 * ROWS, LON), F32), unroll=4)
     inverse = inverse.astype(jnp.int32)
     rows_inv[...] = inverse[:ROWS]
     lanes_inv[...] = inverse[ROWS:]
@@ -244,7 +267,7 @@
         picked[pl.ds(pl.multiple_of(k * 8, 8), 8), :] = pick(fact_rows, 8, rows_fwd, lanes_fwd, k)
         return carry
 
-    lax.fori_loop(0, ROWS, pick_fact, 0)
+    lax.fori_loop(0, ROWS, pick_fact, 0, unroll=4)
     fact_rows[...] = picked[pl.ds(0, 8 * ROWS), :]
 
     @pl.when(jnp.logical_not(has_low))
@@ -275,7 +298,7 @@
                 dst_ref=field.at[slot, :, pl.ds(0, HALF), :],
                 send_sem=high_send,
                 recv_sem=high_recv.at[slot],
-                device_id=(r + 1, m),
+                device_id=above(slot),
                 device_id_type=MESH,
             ).start()
 
@@ -286,7 +309,7 @@
                 dst_ref=field.at[slot, :, pl.ds(HALF + ROWS, HALF), :],
                 send_sem=low_send,
                 recv_sem=low_recv.at[slot],
-                device_id=(r - 1, m),
+                device_id=below(slot),
                 device_id_type=MESH,
             ).start()
 
@@ -318,7 +341,7 @@
             picked[pl.ds(at, MEMBERS), :] = pick(cells, MEMBERS, rows_fwd, lanes_fwd, k)
             return carry
 
-        lax.fori_loop(0, ROWS, pick_patch, 0)
+        lax.fori_loop(0, ROWS, pick_patch, 0, unroll=4)
 
         def quad(q, carry):
             at = pl.multiple_of(q * 4 * MEMBERS, 4 * MEMBERS)
@@ -328,13 +351,16 @@
             cells[pl.ds(at, 4 * MEMBERS), :] = pair_block(picked[pl.ds(at, 4 * MEMBERS), :], truths)
             return carry
 
-        lax.fori_loop(0, ROWS // 4, quad, 0)
+        lax.fori_loop(0, ROWS // 4, quad, 0, unroll=2)
 
         def put_row(row, carry):
-            grad[slot, :, HALF + row, :] = pick(cells, MEMBERS, rows_inv, lanes_inv, row)
-            return carry
-
-        lax.fori_loop(0, ROWS, put_row, 0)
+            at = pl.multiple_of(row * MEMBERS, MEMBERS)
+            mid[pl.ds(at, MEMBERS), :] = pick(cells, MEMBERS, rows_inv, lanes_inv, row)
+            return carry
+
+        lax.fori_loop(0, ROWS, put_row, 0, unroll=4)
+        for member in range(MEMBERS):
+            grad[slot, member, pl.ds(HALF, ROWS), :] = mid[pl.ds(member, ROWS, stride=MEMBERS), :]
 
     def finish(slot):
         wait_halos(grad, slot, down2_recv, up2_recv)
@@ -356,35 +382,35 @@
             ).start()
             return carry
 
-        lax.fori_loop(1, OWNERS, to_peer, 0)
+        lax.fori_loop(1, OWNERS, to_peer, 0, unroll=5)
         pltpu.make_async_copy(
             done.at[slot, pl.ds(2 * m, 2)], out.at[:, variable(slot, m)], ret_recv
         ).start()
 
     def step(i, carry):
-        @pl.when(jnp.logical_and(i >= 3, i < slots + 3))
-        def _():
-            give_back(i - 3)
+        @pl.when(jnp.logical_and(i >= 5, i < slots + 5))
+        def _():
+            give_back(i - 5)
 
         @pl.when(i < slots)
         def _():
             arrive(i)
 
-        @pl.when(jnp.logical_and(i >= 1, i < slots + 1))
-        def _():
-            middle(i - 1)
-
         @pl.when(jnp.logical_and(i >= 2, i < slots + 2))
         def _():
-            finish(i - 2)
-
-        @pl.when(jnp.logical_and(i >= 1, i < slots + 1))
-        def _():
-            send_halos(grad, i - 1, down2_send, down2_recv, up2_send, up2_recv)
+            middle(i - 2)
+
+        @pl.when(jnp.logical_and(i >= 4, i < slots + 4))
+        def _():
+            finish(i - 4)
+
+        @pl.when(jnp.logical_and(i >= 2, i < slots + 2))
+        def _():
+            send_halos(grad, i - 2, down2_send, down2_recv, up2_send, up2_recv)
 
         return carry
 
-    lax.fori_loop(0, SLOTS + 3, step, 0)
+    lax.fori_loop(0, SLOTS + 5, step, 0)
 
     def drain(count):
         pltpu.make_async_copy(

time: 271 us -> 241 us (0.89)
  Pallas kernels: 266 us -> 237 us
    pallas_call x1, Pallas kernels: 266 us -> 237 us  [on_device(): pl.pallas_call(kernel, out_shape=jax.ShapeDtypeStruct((2, V, ROWS, LON),...]
where the time goes in v2:
time: 241 us
  Pallas kernels  237 us (98%)
  local copies, waits for them, and re-layouts  3.96 us (2%)
    pallas_call x1, Pallas kernels, on_device(): pl.pallas_call(kernel, out_shape=jax.ShapeDtypeStruct((2, V, ROWS, LON),...  237 us

profile of v2, /device:TPU:32, one launch (start us, length us, event | category | flops | bytes accessed | tf_op | source)
XLA Modules:
  0.0 241.3 jit_solution(1359903802699251701)
XLA Ops:
  0.0 237.3 %shard_map.55 = f32[2,100,32,128]{3,2,1,0:T(8,128)} custom-call(f32[2,100,32,128]{3,2,1,0:T(8,128)} %x.1, f32[100,32,128]{2,1,0:T(8,128)} %truth.1, s32[32,128]{1,0:T(8,128)} %bitcast.1, bf16[64,192]{1,0:T(8,128)(2,1)} %constant.4.clone.lat, bf16[256,256]{1,0:T(8,128)(2,1)} %constant.5.clone.lon), custom_call_target="tpu_custom_call" | custom-call | tf_op jit(solution)/shard_map/pallas_call | solution.py:450
  237.3 4.0 %copy.7 = f32[2,100,32,128]{3,2,1,0:T(8,128)} copy(f32[2,100,32,128]{3,2,1,0:T(8,128)} %shard_map.55) | data formatting | bytes 6553600

commit v3 on v2

--- a/solution.py
+++ b/solution.py
@@ -219,12 +219,14 @@
 
         return lax.fori_loop(1, OWNERS, to_peer, carry, unroll=5)
 
-    lax.fori_loop(0, SLOTS - 1, send_slot, 0)
-    for index in range(4):
-
-        @pl.when(m != 5 * index)
-        def _(index=index):
-            send_block(SLOTS - 1, 5 * index)
+    lax.fori_loop(0, 1, send_slot, 0)
+
+    def send_slots_tail():
+        for index in range(4):
+
+            @pl.when(m != 5 * index)
+            def _(index=index):
+                send_block(SLOTS - 1, 5 * index)
 
     def keep_slot(slot, carry):
         pltpu.make_async_copy(x.at[:, variable(slot, m)], own_rows(slot), fwd_recv.at[slot]).start()
@@ -388,6 +390,14 @@
         ).start()
 
     def step(i, carry):
+        @pl.when(i + 1 < SLOTS - 1)
+        def _():
+            send_slot(i + 1, 0)
+
+        @pl.when(i + 1 == SLOTS - 1)
+        def _():
+            send_slots_tail()
+
         @pl.when(jnp.logical_and(i >= 5, i < slots + 5))
         def _():
             give_back(i - 5)

time: 241 us -> 213 us (0.88)
  Pallas kernels: 237 us -> 209 us
    pallas_call x1, Pallas kernels: 237 us -> 209 us  [on_device(): pl.pallas_call(kernel, out_shape=jax.ShapeDtypeStruct((2, V, ROWS, LON),...]
where the time goes in v3:
time: 213 us
  Pallas kernels  209 us (98%)
  local copies, waits for them, and re-layouts  3.96 us (2%)
    pallas_call x1, Pallas kernels, on_device(): pl.pallas_call(kernel, out_shape=jax.ShapeDtypeStruct((2, V, ROWS, LON),...  209 us

profile of v3, /device:TPU:32, one launch (start us, length us, event | category | flops | bytes accessed | tf_op | source)
XLA Modules:
  0.0 213.0 jit_solution(3432174863053637622)
XLA Ops:
  0.0 209.1 %shard_map.55 = f32[2,100,32,128]{3,2,1,0:T(8,128)} custom-call(f32[2,100,32,128]{3,2,1,0:T(8,128)} %x.1, f32[100,32,128]{2,1,0:T(8,128)} %truth.1, s32[32,128]{1,0:T(8,128)} %bitcast.1, bf16[64,192]{1,0:T(8,128)(2,1)} %constant.4.clone.lat, bf16[256,256]{1,0:T(8,128)(2,1)} %constant.5.clone.lon), custom_call_target="tpu_custom_call" | custom-call | tf_op jit(solution)/shard_map/pallas_call | solution.py:460
  209.1 4.0 %copy.7 = f32[2,100,32,128]{3,2,1,0:T(8,128)} copy(f32[2,100,32,128]{3,2,1,0:T(8,128)} %shard_map.55) | data formatting | bytes 6553600

commit v4 on v3

--- a/solution.py
+++ b/solution.py
@@ -19,6 +19,13 @@
 SLOTS = 7
 SPAN = ROWS + 2 * HALF
 CELLS = ROWS * LON
+TOP = REGIONS // 2 - 1
+UP_RELAYS = (4, 2)
+DOWN_RELAYS = (11, 13)
+RELAYS = 2
+AWAY = 0
+PIECE = 10
+STRAIGHT = MEMBERS - RELAYS * PIECE
 MESH = pl.DeviceIdType.MESH
 F32 = jnp.float32
 BF16 = jnp.bfloat16
@@ -151,6 +158,7 @@
     raw, grad, done, mid, cells, picked, facts, fact_rows, rows_fwd, lanes_fwd, rows_inv, lanes_inv,
     fwd_send, fwd_recv, up_send, up_recv, down_send, down_recv,
     up2_send, up2_recv, down2_send, down2_recv, ret_send, ret_recv, fact_sem,
+    way, way2, way_send, way_recv, way2_send, way2_recv,
 ):
     r = lax.axis_index("region")
     m = lax.axis_index("member")
@@ -187,17 +195,37 @@
     def _():
         pl.semaphore_signal(barrier, inc=1, device_id=(r + 1, m), device_id_type=MESH)
 
-    @pl.when(r == REGIONS // 2 - 1)
-    def _():
-        pl.semaphore_signal(barrier, inc=1, device_id=above(1), device_id_type=MESH)
-
-    @pl.when(r == REGIONS // 2)
-    def _():
-        pl.semaphore_signal(barrier, inc=1, device_id=below(1), device_id_type=MESH)
-
-    crossing = jnp.logical_or(r == REGIONS // 2 - 1, r == REGIONS // 2)
-    neighbours = has_low.astype(jnp.int32) + has_high.astype(jnp.int32) + crossing.astype(jnp.int32)
-    pl.semaphore_wait(barrier, OWNERS - 1 + neighbours)
+    relay_up = jnp.logical_or(r == UP_RELAYS[0], r == UP_RELAYS[1])
+    relay_down = jnp.logical_or(r == DOWN_RELAYS[0], r == DOWN_RELAYS[1])
+    at_top = r == TOP
+    at_bottom = r == TOP + 1
+    ahead = turned(m, 1)
+    behind = turned(m, -1)
+
+    def greet(condition, peers):
+        @pl.when(condition)
+        def _():
+            for peer in peers:
+                pl.semaphore_signal(barrier, inc=1, device_id=peer, device_id_type=MESH)
+
+        return condition.astype(jnp.int32) * len(peers)
+
+    greeted = has_low.astype(jnp.int32) + has_high.astype(jnp.int32)
+    greeted += greet(
+        at_top,
+        [(TOP + 1, behind)]
+        + [(region, m) for region in UP_RELAYS]
+        + [(region, who) for region in DOWN_RELAYS for who in (m, behind)],
+    )
+    greeted += greet(
+        at_bottom,
+        [(TOP, ahead)]
+        + [(region, m) for region in DOWN_RELAYS]
+        + [(region, who) for region in UP_RELAYS for who in (m, ahead)],
+    )
+    greeted += greet(relay_up, [(TOP, m), (TOP + 1, m), (TOP + 1, behind)])
+    greeted += greet(relay_down, [(TOP + 1, m), (TOP, m), (TOP, ahead)])
+    pl.semaphore_wait(barrier, OWNERS - 1 + greeted)
 
     def own_rows(slot):
         return raw.at[slot, pl.ds(2 * m, 2), pl.ds(HALF, ROWS), :]
@@ -290,30 +318,60 @@
 
         lax.fori_loop(0, slots, clear, 0)
 
-    def send_halos(field, slot, low_send, low_recv, high_send, high_recv):
-        middle = field.at[slot, :, pl.ds(HALF, ROWS), :]
+    def push(source, target, send, recv, device):
+        pltpu.make_async_remote_copy(
+            src_ref=source,
+            dst_ref=target,
+            send_sem=send,
+            recv_sem=recv,
+            device_id=device,
+            device_id_type=MESH,
+        ).start()
+
+    def send_halos(field, slot, low_send, low_recv, high_send, high_recv, stop, stop_recv):
+        def piece(first, count, row):
+            return field.at[slot, pl.ds(first, count), pl.ds(row, ROWS), :]
+
+        def out_to(device, regions, row, send, recv, crossing):
+            @pl.when(jnp.logical_not(crossing))
+            def _():
+                push(piece(0, MEMBERS, HALF), piece(0, MEMBERS, row), send, recv, device)
+
+            @pl.when(crossing)
+            def _():
+                for n, region in enumerate(regions):
+                    source = piece(STRAIGHT + n * PIECE, PIECE, HALF)
+                    push(source, stop.at[slot], send, stop_recv.at[slot], (region, m))
+                push(piece(0, STRAIGHT, HALF), piece(0, STRAIGHT, row), send, recv, device)
 
         @pl.when(has_high)
         def _():
-            pltpu.make_async_remote_copy(
-                src_ref=middle,
-                dst_ref=field.at[slot, :, pl.ds(0, HALF), :],
-                send_sem=high_send,
-                recv_sem=high_recv.at[slot],
-                device_id=above(slot),
-                device_id_type=MESH,
-            ).start()
+            out_to(above(slot), UP_RELAYS, 0, high_send, high_recv.at[slot], at_top)
 
         @pl.when(has_low)
         def _():
-            pltpu.make_async_remote_copy(
-                src_ref=middle,
-                dst_ref=field.at[slot, :, pl.ds(HALF + ROWS, HALF), :],
-                send_sem=low_send,
-                recv_sem=low_recv.at[slot],
-                device_id=below(slot),
-                device_id_type=MESH,
-            ).start()
+            out_to(
+                below(slot), DOWN_RELAYS, HALF + ROWS, low_send, low_recv.at[slot], at_bottom
+            )
+
+    def pass_on(field, slot, low_recv, high_recv, stop, stop_send, stop_recv):
+        def forward(n, row, recv, device):
+            part = stop.at[slot]
+            pltpu.make_async_copy(part, part, stop_recv.at[slot]).wait()
+            target = field.at[slot, pl.ds(STRAIGHT + n * PIECE, PIECE), pl.ds(row, HALF), :]
+            push(part, target, stop_send, recv.at[slot], device)
+
+        odd = lax.rem(slot, 2) == 1
+
+        @pl.when(relay_up)
+        def _():
+            owner = jnp.where(odd, behind, m)
+            forward((r == UP_RELAYS[1]).astype(jnp.int32), 0, high_recv, (TOP + 1, owner))
+
+        @pl.when(relay_down)
+        def _():
+            owner = jnp.where(odd, ahead, m)
+            forward((r == DOWN_RELAYS[1]).astype(jnp.int32), HALF + ROWS, low_recv, (TOP, owner))
 
     def wait_halos(field, slot, low_recv, high_recv):
         @pl.when(has_low)
@@ -329,7 +387,7 @@
     def arrive(slot):
         part = raw.at[slot, :, pl.ds(HALF, ROWS), :]
         pltpu.make_async_copy(part, part, fwd_recv.at[slot]).wait()
-        send_halos(raw, slot, down_send, down_recv, up_send, up_recv)
+        send_halos(raw, slot, down_send, down_recv, up_send, up_recv, way, way_recv)
 
     def middle(slot):
         wait_halos(raw, slot, down_recv, up_recv)
@@ -410,13 +468,21 @@
         def _():
             middle(i - 2)
 
+        @pl.when(i < slots)
+        def _():
+            pass_on(raw, i, down_recv, up_recv, way, way_send, way_recv)
+
+        @pl.when(jnp.logical_and(i >= 3, i < slots + 3))
+        def _():
+            pass_on(grad, i - 3, down2_recv, up2_recv, way2, way2_send, way2_recv)
+
         @pl.when(jnp.logical_and(i >= 4, i < slots + 4))
         def _():
             finish(i - 4)
 
         @pl.when(jnp.logical_and(i >= 2, i < slots + 2))
         def _():
-            send_halos(grad, i - 2, down2_send, down2_recv, up2_send, up2_recv)
+            send_halos(grad, i - 2, down2_send, down2_recv, up2_send, up2_recv, way2, way2_recv)
 
         return carry
 
@@ -428,6 +494,12 @@
         ).wait()
         sent = done.at[pl.ds(0, count), pl.ds(0, 2 * OWNERS - 2)]
         pltpu.make_async_copy(sent, sent, ret_send).wait()
+
+        @pl.when(jnp.logical_or(relay_up, relay_down))
+        def _():
+            for field, sem in ((way, way_send), (way2, way2_send)):
+                part = field.at[pl.ds(0, count)]
+                pltpu.make_async_copy(part, part, sem).wait()
 
         @pl.when(has_high)
         def _():
@@ -477,6 +549,9 @@
             pltpu.VMEM((ROWS, LON), jnp.int32),
             dma(()), dma((SLOTS,)), dma(()), dma((SLOTS,)), dma(()), dma((SLOTS,)),
             dma(()), dma((SLOTS,)), dma(()), dma((SLOTS,)), dma(()), dma(()), dma(()),
+            pltpu.VMEM((SLOTS, PIECE, HALF, LON), F32),
+            pltpu.VMEM((SLOTS, PIECE, HALF, LON), F32),
+            dma(()), dma((SLOTS,)), dma(()), dma((SLOTS,)),
         ],
         compiler_params=pltpu.CompilerParams(
             collective_id=0, has_side_effects=True, vmem_limit_bytes=56 * 1024 * 1024

time: 213 us -> 207 us (0.972); the launches traced: 213 us -> 204 us
  Pallas kernels: 209 us -> 200 us
    pallas_call x1, Pallas kernels: 209 us -> 200 us  [on_device(): pl.pallas_call(kernel, out_shape=jax.ShapeDtypeStruct((2, V, ROWS, LON),...]
where the time goes in v4:
time: 207 us; the launch traced here: 204 us
  Pallas kernels  200 us (97%)
  local copies, waits for them, and re-layouts  3.96 us (2%)
    pallas_call x1, Pallas kernels, on_device(): pl.pallas_call(kernel, out_shape=jax.ShapeDtypeStruct((2, V, ROWS, LON),...  200 us

profile of v4, /device:TPU:32, one launch (start us, length us, event | category | flops | bytes accessed | tf_op | source)
XLA Modules:
  0.0 203.9 jit_solution(17329614774131296549)
XLA Ops:
  0.0 199.9 %shard_map.55 = f32[2,100,32,128]{3,2,1,0:T(8,128)} custom-call(f32[2,100,32,128]{3,2,1,0:T(8,128)} %x.1, f32[100,32,128]{2,1,0:T(8,128)} %truth.1, s32[32,128]{1,0:T(8,128)} %bitcast.1, bf16[64,192]{1,0:T(8,128)(2,1)} %constant.4.clone.lat, bf16[256,256]{1,0:T(8,128)(2,1)} %constant.5.clone.lon), custom_call_target="tpu_custom_call" | custom-call | tf_op jit(solution)/shard_map/pallas_call | solution.py:532
  199.9 4.0 %copy.7 = f32[2,100,32,128]{3,2,1,0:T(8,128)} copy(f32[2,100,32,128]{3,2,1,0:T(8,128)} %shard_map.55) | data formatting | bytes 6553600

commit v5 on v4

--- a/solution.py
+++ b/solution.py
@@ -460,13 +460,17 @@
         def _():
             give_back(i - 5)
 
-        @pl.when(i < slots)
+        @pl.when(jnp.logical_and(i < slots, i != 2))
         def _():
             arrive(i)
 
         @pl.when(jnp.logical_and(i >= 2, i < slots + 2))
         def _():
             middle(i - 2)
+
+        @pl.when(i == 2)
+        def _():
+            arrive(i)
 
         @pl.when(i < slots)
         def _():

time: 207 us -> 203 us (0.981); the launches traced: 204 us -> 203 us
  no operation moved by 1% of the time
where the time goes in v5:
time: 203 us
  Pallas kernels  199 us (98%)
  local copies, waits for them, and re-layouts  3.96 us (2%)
    pallas_call x1, Pallas kernels, on_device(): pl.pallas_call(kernel, out_shape=jax.ShapeDtypeStruct((2, V, ROWS, LON),...  199 us

profile of v5, /device:TPU:32, one launch (start us, length us, event | category | flops | bytes accessed | tf_op | source)
XLA Modules:
  0.0 202.6 jit_solution(5346253563118377813)
XLA Ops:
  0.0 198.7 %shard_map.55 = f32[2,100,32,128]{3,2,1,0:T(8,128)} custom-call(f32[2,100,32,128]{3,2,1,0:T(8,128)} %x.1, f32[100,32,128]{2,1,0:T(8,128)} %truth.1, s32[32,128]{1,0:T(8,128)} %bitcast.1, bf16[64,192]{1,0:T(8,128)(2,1)} %constant.4.clone.lat, bf16[256,256]{1,0:T(8,128)(2,1)} %constant.5.clone.lon), custom_call_target="tpu_custom_call" | custom-call | tf_op jit(solution)/shard_map/pallas_call | solution.py:536
  198.7 4.0 %copy.7 = f32[2,100,32,128]{3,2,1,0:T(8,128)} copy(f32[2,100,32,128]{3,2,1,0:T(8,128)} %shard_map.55) | data formatting | bytes 6553600

commit v6 on v5

--- a/solution.py
+++ b/solution.py
@@ -24,7 +24,7 @@
 DOWN_RELAYS = (11, 13)
 RELAYS = 2
 AWAY = 0
-PIECE = 10
+PIECE = 12
 STRAIGHT = MEMBERS - RELAYS * PIECE
 MESH = pl.DeviceIdType.MESH
 F32 = jnp.float32

time: 203 us -> 208 us (1.025); the launches traced: 203 us -> 205 us
    pallas_call x1, Pallas kernels: 199 us -> 201 us  [on_device(): pl.pallas_call(kernel, out_shape=jax.ShapeDtypeStruct((2, V, ROWS, LON),...]
where the time goes in v6:
time: 208 us; the launch traced here: 205 us
  Pallas kernels  201 us (97%)
  local copies, waits for them, and re-layouts  3.96 us (2%)
    pallas_call x1, Pallas kernels, on_device(): pl.pallas_call(kernel, out_shape=jax.ShapeDtypeStruct((2, V, ROWS, LON),...  201 us

profile of v6, /device:TPU:32, one launch (start us, length us, event | category | flops | bytes accessed | tf_op | source)
XLA Modules:
  0.0 204.7 jit_solution(11120111383738403257)
XLA Ops:
  0.0 200.8 %shard_map.55 = f32[2,100,32,128]{3,2,1,0:T(8,128)} custom-call(f32[2,100,32,128]{3,2,1,0:T(8,128)} %x.1, f32[100,32,128]{2,1,0:T(8,128)} %truth.1, s32[32,128]{1,0:T(8,128)} %bitcast.1, bf16[64,192]{1,0:T(8,128)(2,1)} %constant.4.clone.lat, bf16[256,256]{1,0:T(8,128)(2,1)} %constant.5.clone.lon), custom_call_target="tpu_custom_call" | custom-call | tf_op jit(solution)/shard_map/pallas_call | solution.py:536
  200.8 4.0 %copy.7 = f32[2,100,32,128]{3,2,1,0:T(8,128)} copy(f32[2,100,32,128]{3,2,1,0:T(8,128)} %shard_map.55) | data formatting | bytes 6553600
